TPU v7x, 32 devices: a whole 2x2x4 slice. The times are simulated.
32 devices in a mesh: fx: 8 (over z, x), fy: 4 (over y, core).
Axes of the slice: x: 2, y: 2, z: 4, core: 2. Of those that a mesh axis runs over, the one named last changes fastest.
Arguments:
- right_side: float32 [512, 2048], P(('fx', 'fy'))
- coupling: float32 [512, 11, 4096], P(('fx', 'fy')), may hold values from -0.109375 to 0.109375
- face_columns: int32 [512, 11], P(('fx', 'fy')), may hold values from 0 to 31, as said below
- ghost_lists: int32 [128, 4], P(('fx', 'fy')), may hold values from 0 to 15, as said below
Outputs:
- solution: float32 [512, 2048], P(('fx', 'fy'))
- residual: float32 [512, 2048], P(('fx', 'fy'))
Inputs may be any that keep to these rules, and one draw needn't show every extreme that they name: face_columns[f, 0] is f's own index within its block; entries 1 to 6 name other faces of the same block, all distinct and below 16; entries 7 to 10 are distinct and name received faces, 16 + d * 4 + g for the g-th face of group d of the extended list; every received slot of every block is named by some row of that block. `ghost_lists`: each row names 4 distinct faces of its block by local index.
All inputs are finite; a program needn't handle non-finite values.
Results may differ from a plain program's by a relative error of at most 0.0003.
Values sent between devices are 32-bit elements; how exact they have to be, the bound alone decides.
A program may use at most 64 MiB of HBM per device.

v0:
```python
import jax
import jax.numpy as jnp
from jax import lax
from jax.sharding import PartitionSpec as P

DOF = 64
NRHS = 32
BLOCKS = 11
POWERS = 3


def from_behind(block, axis, distance):
    devices = range(lax.axis_size(axis))
    route = [(i - distance, i) for i in devices if i - distance in devices]
    return lax.ppermute(block, axis, route)


def receive_rows(field, ghost_lists):
    from_lower_x = from_behind(jnp.take(field, ghost_lists[1], axis=0), "fx", 1)
    from_upper_x = from_behind(jnp.take(field, ghost_lists[0], axis=0), "fx", -1)
    from_lower_y = from_behind(jnp.take(field, ghost_lists[3], axis=0), "fy", 1)
    from_upper_y = from_behind(jnp.take(field, ghost_lists[2], axis=0), "fy", -1)
    return jnp.concatenate([from_lower_x, from_upper_x, from_lower_y, from_upper_y], axis=0)


def contract(block_mats, picked):
    face_count = picked.shape[0]
    shaped = picked.reshape(face_count, picked.shape[1], DOF, NRHS)
    result = jnp.einsum("fkab,fkbr->far", block_mats, shaped, precision=lax.Precision.HIGHEST)
    return result.reshape(face_count, DOF * NRHS)


def solve_small(gram_total):
    count = NRHS
    row_ids = jnp.arange((POWERS + 1) * count)[:, None]
    col_ids = jnp.arange(POWERS * count)[None, :]
    shift_map = ((row_ids == col_ids) | (row_ids == col_ids + count)).astype(jnp.float32)
    first = (row_ids == jnp.arange(count)[None, :]).astype(jnp.float32)
    high = lax.Precision.HIGHEST
    normal_matrix = jnp.dot(
        shift_map.T, jnp.dot(gram_total, shift_map, precision=high), precision=high
    )
    right_terms = jnp.dot(shift_map.T, gram_total[:, :count], precision=high)
    factor = jnp.linalg.cholesky(normal_matrix)
    coeffs = jax.scipy.linalg.cho_solve((factor, True), right_terms)
    combo = first - jnp.dot(shift_map, coeffs, precision=high)
    return (coeffs, combo)


def on_device(right_side, coupling, face_columns, ghost_lists):
    face_count = right_side.shape[0]
    block_mats = coupling.reshape(face_count, BLOCKS, DOF, DOF)
    high = lax.Precision.HIGHEST

    def as_rows(field):
        return field.reshape(face_count * DOF, NRHS)

    fields = [right_side]
    partial_grams = []
    for power_index in range(POWERS + 1):
        if power_index > 0:
            power_field = fields[-1]
            received = receive_rows(power_field, ghost_lists)
            extended = jnp.concatenate([power_field, received], axis=0)
            fields.append(contract(block_mats, jnp.take(extended, face_columns, axis=0)))
        earlier_rows = jnp.concatenate([as_rows(item) for item in fields], axis=1)
        local_block = jnp.dot(
            earlier_rows.T, as_rows(fields[-1]), precision=high, preferred_element_type=jnp.float32
        )
        partial_grams.append(lax.psum(local_block, ("fx", "fy")))
    total_cols = (POWERS + 1) * NRHS
    upper_part = jnp.concatenate(
        [
            jnp.concatenate(
                [item, jnp.zeros((total_cols - item.shape[0], NRHS), jnp.float32)], axis=0
            )
            for item in partial_grams
        ],
        axis=1,
    )
    block_index = jnp.arange(total_cols) // NRHS
    gram_total = jnp.where(block_index[:, None] <= block_index[None, :], upper_part, upper_part.T)
    stacked = jnp.concatenate([as_rows(item) for item in fields], axis=1)
    coeffs, combo = solve_small(gram_total)
    solution = jnp.dot(stacked[:, : POWERS * NRHS], coeffs, precision=high)
    residual = jnp.dot(stacked, combo, precision=high)
    return (solution.reshape(face_count, DOF * NRHS), residual.reshape(face_count, DOF * NRHS))


def solution(mesh):
    placed = (
        P(("fx", "fy"), None),
        P(("fx", "fy"), None, None),
        P(("fx", "fy"), None),
        P(("fx", "fy"), None),
    )
    return jax.shard_map(
        on_device,
        mesh=mesh,
        in_specs=placed,
        out_specs=(P(("fx", "fy"), None), P(("fx", "fy"), None)),
        check_vma=False,
    )
```

profile of v0, /device:TPU:0, one launch (start us, length us, event | category | flops | bytes accessed | tf_op | source)
XLA Modules:
  0.0 199.0 jit_solution(18109654426102840548)
XLA Ops:
  0.6 0.8 compare_and_fusion.1
  1.5 1.5 gather_fusion
  3.1 4.9 %collective-permute-start = (f32[4,2048]{1,0:T(4,128)S(1)}, f32[4,2048]{1,0:T(4,128)S(1)}, u32[]{:S(2)}, u32[]{:S(2)}) collective-permute-start(f32[4,2048]{1,0:T(4,128)S(1)} %broadcast_select_fusion.14), channel_id=1, source_target_pairs={{0,4},{4,8},{8,12},{12,16},{16,20},{20,24},{24,28},{1,5},{5,9},{9,... | collective-permute-start | bytes 98312 | tf_op jit(solution)/shard_map/ppermute | solution.py:15
  7.9 1.5 gather_fusion.1
  9.5 1.3 collective-permute-start.1
  10.8 1.5 gather_fusion.2
  12.4 1.4 collective-permute-start.2
  13.9 1.5 gather_fusion.3
  15.4 1.3 collective-permute-start.3
  16.7 0.7 compare_select_fusion
  17.4 0.7 compare_and_fusion
  18.1 1.1 reshape.90
  19.3 1.0 fusion.40
  20.3 5.7 %reshape.92 = f32[16,11,64,64]{3,2,0,1:T(8,128)} reshape(f32[16,11,4096]{2,0,1:T(8,128)} %param.9) | data formatting | bytes 5767168 | tf_op jit(solution)/shard_map/reshape | solution.py:52
  26.2 1.2 gather_fusion.4
  27.3 1.5 reshape.248
  28.9 1.8 broadcast_select_fusion.2
  30.7 3.6 %reshape.276 = f32[16,11,64,32]{3,2,1,0:T(8,128)} reshape(f32[16,11,2048]{2,1,0:T(8,128)S(1)} %broadcast_select_fusion.2) | data formatting | bytes 2883584 | tf_op jit(solution)/shard_map/reshape | solution.py:28
  34.2 12.0 %fusion.6 = f32[16,64,32]{1,2,0:T(8,128)S(1)} fusion(f32[16,11,64,64]{3,2,0,1:T(8,128)} %reshape.92, f32[16,11,64,32]{3,2,1,0:T(8,128)} %reshape.276), kind=kOutput, calls=%fused_computation.21 | convolution fusion | flops 276824064 | bytes 4456448 | tf_op jit(solution)/shard_map/fkab,fkbr->far/dot_general | solution.py:29
  46.5 0.2 reshape.93
  46.7 0.6 gather_fusion.6
  47.3 0.6 gather_fusion.7
  47.9 0.6 gather_fusion.8
  48.4 0.6 gather_fusion.5
  49.3 1.3 collective-permute-start.5
  50.6 4.6 %collective-permute-start.6 = (f32[4,2048]{1,0:T(4,128)S(1)}, f32[4,2048]{1,0:T(4,128)S(1)}, u32[]{:S(2)}, u32[]{:S(2)}) collective-permute-start(f32[4,2048]{1,0:T(4,128)S(1)} %broadcast_select_fusion.8), channel_id=1, source_target_pairs={{0,1},{1,2},{2,3},{4,5},{5,6},{6,7},{8,9},{9,10},{10,11},{12,13},{... | collective-permute-start | bytes 98312 | tf_op jit(solution)/shard_map/ppermute | solution.py:15
  55.3 1.3 collective-permute-start.7
  56.7 5.3 %collective-permute-start.4 = (f32[4,2048]{1,0:T(4,128)S(1)}, f32[4,2048]{1,0:T(4,128)S(1)}, u32[]{:S(2)}, u32[]{:S(2)}) collective-permute-start(f32[4,2048]{1,0:T(4,128)S(1)} %broadcast_select_fusion.10), channel_id=1, source_target_pairs={{0,4},{4,8},{8,12},{12,16},{16,20},{20,24},{24,28},{1,5},{5,9},{9,... | collective-permute-start | bytes 98312 | tf_op jit(solution)/shard_map/ppermute | solution.py:15
  62.4 1.1 fusion.15
  63.6 1.2 gather_fusion.9
  64.8 1.5 reshape.260
  66.3 1.8 broadcast_select_fusion.1
  68.1 3.6 %reshape.277 = f32[16,11,64,32]{3,2,1,0:T(8,128)} reshape(f32[16,11,2048]{2,1,0:T(8,128)S(1)} %broadcast_select_fusion.1) | data formatting | bytes 2883584 | tf_op jit(solution)/shard_map/reshape | solution.py:28
  71.7 12.0 %fusion.9 = f32[16,64,32]{1,2,0:T(8,128)S(1)} fusion(f32[16,11,64,64]{3,2,0,1:T(8,128)} %reshape.92, f32[16,11,64,32]{3,2,1,0:T(8,128)} %reshape.277), kind=kOutput, calls=%fused_computation.22 | convolution fusion | flops 276824064 | bytes 4456448 | tf_op jit(solution)/shard_map/fkab,fkbr->far/dot_general | solution.py:29
  83.9 0.2 reshape.95
  84.2 0.6 gather_fusion.12
  84.8 0.6 gather_fusion.13
  85.3 0.6 gather_fusion.10
  85.9 0.6 gather_fusion.11
  86.7 4.0 %collective-permute-start.10 = (f32[4,2048]{1,0:T(4,128)S(1)}, f32[4,2048]{1,0:T(4,128)S(1)}, u32[]{:S(2)}, u32[]{:S(2)}) collective-permute-start(f32[4,2048]{1,0:T(4,128)S(1)} %broadcast_select_fusion.4), channel_id=1, source_target_pairs={{0,1},{1,2},{2,3},{4,5},{5,6},{6,7},{8,9},{9,10},{10,11},{12,13},{... | collective-permute-start | bytes 98312 | tf_op jit(solution)/shard_map/ppermute | solution.py:15
  90.8 1.3 collective-permute-start.11
  92.2 4.8 %collective-permute-start.8 = (f32[4,2048]{1,0:T(4,128)S(1)}, f32[4,2048]{1,0:T(4,128)S(1)}, u32[]{:S(2)}, u32[]{:S(2)}) collective-permute-start(f32[4,2048]{1,0:T(4,128)S(1)} %broadcast_select_fusion.6), channel_id=1, source_target_pairs={{0,4},{4,8},{8,12},{12,16},{16,20},{20,24},{24,28},{1,5},{5,9},{9,... | collective-permute-start | bytes 98312 | tf_op jit(solution)/shard_map/ppermute | solution.py:15
  97.1 1.5 collective-permute-start.9
  98.9 1.3 fusion.39
  100.2 2.8 %collective-permute-done.9 = f32[4,2048]{1,0:T(4,128)S(1)} collective-permute-done((f32[4,2048]{1,0:T(4,128)S(1)}, f32[4,2048]{1,0:T(4,128)S(1)}, u32[]{:S(2)}, u32[]{:S(2)}) %collective-permute-start.9) | collective-permute-done | bytes 32800 | tf_op jit(solution)/shard_map/ppermute | solution.py:15
  103.1 1.2 gather_fusion.14
  104.3 1.6 reshape.272
  105.9 3.2 %broadcast_select_fusion = f32[16,11,2048]{2,1,0:T(8,128)} fusion(f32[16,11,2048]{2,1,0:T(8,128)} %reshape.272, pred[16,11]{1,0:T(8,128)(4,1)S(1)} %compare_and_fusion), kind=kLoop, calls=%fused_computation.25 | loop fusion | flops 360448 | bytes 2883760 | tf_op jit(solution)/shard_map/jit(_take)/select_n | solution.py:65
  109.2 5.2 %reshape.278 = f32[16,11,64,32]{3,2,1,0:T(8,128)} reshape(f32[16,11,2048]{2,1,0:T(8,128)} %broadcast_select_fusion) | data formatting | bytes 2883584 | tf_op jit(solution)/shard_map/reshape | solution.py:28
  114.3 12.0 %fusion.12 = f32[16,64,32]{1,2,0:T(8,128)S(1)} fusion(f32[16,11,64,64]{3,2,0,1:T(8,128)} %reshape.92, f32[16,11,64,32]{3,2,1,0:T(8,128)} %reshape.278), kind=kOutput, calls=%fused_computation.23 | convolution fusion | flops 276824064 | bytes 4456448 | tf_op jit(solution)/shard_map/fkab,fkbr->far/dot_general | solution.py:29
  126.9 0.5 pad_maximum_fusion.1
  127.3 1.0 fusion.41
  128.3 48.2 %all-reduce.3 = (f32[96,32]{1,0:T(8,128)S(1)}, f32[64,32]{1,0:T(8,128)S(1)}, f32[32,32]{1,0:T(8,128)S(1)}, f32[128,32]{1,0:T(8,128)S(1)}) all-reduce(f32[96,32]{1,0:T(8,128)S(1)} %fusion.39, f32[64,32]{1,0:T(8,128)S(1)} %fusion.15, f32[32,32]{1,0:T(8,128)S(1)} %fusion.40, ...), channel_id=1, replica_groups=mesh['fx'=8,'fy'=4] {'fx','fy'}, use_global_device_ids=true, to_apply=%region_2.5 | all-reduce | flops 10240 | bytes 81920 | tf_op jit(solution)/shard_map/psum | solution.py:70
  177.1 0.2 fusion.19
  177.3 0.2 fusion.33
  177.7 8.8 %cholesky.16 = f32[96,96]{1,0:T(8,128)S(1)} custom-call(f32[96,96]{1,0:T(8,128)S(1)} %fusion.30), custom_call_target="Cholesky" | custom-call | tf_op jit(solution)/shard_map/jit(cholesky)/cholesky | solution.py:44
  186.5 0.6 compare_reduce_fusion
  187.2 0.7 fusion.25
  187.8 7.4 %custom-call.10 = f32[1,96,96]{1,2,0:T(8,128)S(1)} custom-call(f32[1,96,96]{2,1,0:T(8,128)S(1)} %fusion.25), custom_call_target="InvertDiagBlocksLowerTriangular" | custom-call | tf_op jit(solution)/shard_map/jit(_cho_solve)/triangular_solve | solution.py:45
  195.2 0.3 fusion.28
  195.9 0.7 fusion.38
  196.6 0.6 fusion.42
  197.2 0.9 reshape.98
  198.1 0.9 reshape.97
  (56 shorter events, 4.2 us)
Async XLA Ops:
  3.1 23.0 %collective-permute-start = (f32[4,2048]{1,0:T(4,128)S(1)}, f32[4,2048]{1,0:T(4,128)S(1)}, u32[]{:S(2)}, u32[]{:S(2)}) collective-permute-start(f32[4,2048]{1,0:T(4,128)S(1)} %broadcast_select_fusion.14), channel_id=1, source_target_pairs={{0,4},{4,8},{8,12},{12,16},{16,20},{20,24},{24,28},{1,5},{5,9},{9,... | collective-permute-start | bytes 98312 | tf_op jit(solution)/shard_map/ppermute | solution.py:15
  9.5 16.5 %collective-permute-start.1 = (f32[4,2048]{1,0:T(4,128)S(1)}, f32[4,2048]{1,0:T(4,128)S(1)}, u32[]{:S(2)}, u32[]{:S(2)}) collective-permute-start(f32[4,2048]{1,0:T(4,128)S(1)} %broadcast_select_fusion.13), channel_id=1, source_target_pairs={{4,0},{8,4},{12,8},{16,12},{20,16},{24,20},{28,24},{5,1},{9,5},{13... | collective-permute-start | bytes 98312 | tf_op jit(solution)/shard_map/ppermute | solution.py:15
  12.4 13.7 %collective-permute-start.2 = (f32[4,2048]{1,0:T(4,128)S(1)}, f32[4,2048]{1,0:T(4,128)S(1)}, u32[]{:S(2)}, u32[]{:S(2)}) collective-permute-start(f32[4,2048]{1,0:T(4,128)S(1)} %broadcast_select_fusion.12), channel_id=1, source_target_pairs={{0,1},{1,2},{2,3},{4,5},{5,6},{6,7},{8,9},{9,10},{10,11},{12,13},{... | collective-permute-start | bytes 98312 | tf_op jit(solution)/shard_map/ppermute | solution.py:15
  15.4 10.6 %collective-permute-start.3 = (f32[4,2048]{1,0:T(4,128)S(1)}, f32[4,2048]{1,0:T(4,128)S(1)}, u32[]{:S(2)}, u32[]{:S(2)}) collective-permute-start(f32[4,2048]{1,0:T(4,128)S(1)} %broadcast_select_fusion.11), channel_id=1, source_target_pairs={{1,0},{2,1},{3,2},{5,4},{6,5},{7,6},{9,8},{10,9},{11,10},{13,12},{... | collective-permute-start | bytes 98312 | tf_op jit(solution)/shard_map/ppermute | solution.py:15
  20.3 5.8 %copy-start = (f32[16,2048]{1,0:T(8,128)S(1)}, f32[16,2048]{1,0:T(8,128)}, u32[]{:S(2)}) copy-start(f32[16,2048]{1,0:T(8,128)} %param.8) | copy-start | bytes 393220
  49.3 14.3 %collective-permute-start.5 = (f32[4,2048]{1,0:T(4,128)S(1)}, f32[4,2048]{1,0:T(4,128)S(1)}, u32[]{:S(2)}, u32[]{:S(2)}) collective-permute-start(f32[4,2048]{1,0:T(4,128)S(1)} %broadcast_select_fusion.9), channel_id=1, source_target_pairs={{4,0},{8,4},{12,8},{16,12},{20,16},{24,20},{28,24},{5,1},{9,5},{13... | collective-permute-start | bytes 98312 | tf_op jit(solution)/shard_map/ppermute | solution.py:15
  50.6 12.9 %collective-permute-start.6 = (f32[4,2048]{1,0:T(4,128)S(1)}, f32[4,2048]{1,0:T(4,128)S(1)}, u32[]{:S(2)}, u32[]{:S(2)}) collective-permute-start(f32[4,2048]{1,0:T(4,128)S(1)} %broadcast_select_fusion.8), channel_id=1, source_target_pairs={{0,1},{1,2},{2,3},{4,5},{5,6},{6,7},{8,9},{9,10},{10,11},{12,13},{... | collective-permute-start | bytes 98312 | tf_op jit(solution)/shard_map/ppermute | solution.py:15
  55.3 8.2 %collective-permute-start.7 = (f32[4,2048]{1,0:T(4,128)S(1)}, f32[4,2048]{1,0:T(4,128)S(1)}, u32[]{:S(2)}, u32[]{:S(2)}) collective-permute-start(f32[4,2048]{1,0:T(4,128)S(1)} %broadcast_select_fusion.7), channel_id=1, source_target_pairs={{1,0},{2,1},{3,2},{5,4},{6,5},{7,6},{9,8},{10,9},{11,10},{13,12},{... | collective-permute-start | bytes 98312 | tf_op jit(solution)/shard_map/ppermute | solution.py:15
  56.7 6.9 %collective-permute-start.4 = (f32[4,2048]{1,0:T(4,128)S(1)}, f32[4,2048]{1,0:T(4,128)S(1)}, u32[]{:S(2)}, u32[]{:S(2)}) collective-permute-start(f32[4,2048]{1,0:T(4,128)S(1)} %broadcast_select_fusion.10), channel_id=1, source_target_pairs={{0,4},{4,8},{8,12},{12,16},{16,20},{20,24},{24,28},{1,5},{5,9},{9,... | collective-permute-start | bytes 98312 | tf_op jit(solution)/shard_map/ppermute | solution.py:15
  86.7 13.5 %collective-permute-start.10 = (f32[4,2048]{1,0:T(4,128)S(1)}, f32[4,2048]{1,0:T(4,128)S(1)}, u32[]{:S(2)}, u32[]{:S(2)}) collective-permute-start(f32[4,2048]{1,0:T(4,128)S(1)} %broadcast_select_fusion.4), channel_id=1, source_target_pairs={{0,1},{1,2},{2,3},{4,5},{5,6},{6,7},{8,9},{9,10},{10,11},{12,13},{... | collective-permute-start | bytes 98312 | tf_op jit(solution)/shard_map/ppermute | solution.py:15
  90.8 9.4 %collective-permute-start.11 = (f32[4,2048]{1,0:T(4,128)S(1)}, f32[4,2048]{1,0:T(4,128)S(1)}, u32[]{:S(2)}, u32[]{:S(2)}) collective-permute-start(f32[4,2048]{1,0:T(4,128)S(1)} %broadcast_select_fusion.3), channel_id=1, source_target_pairs={{1,0},{2,1},{3,2},{5,4},{6,5},{7,6},{9,8},{10,9},{11,10},{13,12},{... | collective-permute-start | bytes 98312 | tf_op jit(solution)/shard_map/ppermute | solution.py:15
  92.2 8.1 %collective-permute-start.8 = (f32[4,2048]{1,0:T(4,128)S(1)}, f32[4,2048]{1,0:T(4,128)S(1)}, u32[]{:S(2)}, u32[]{:S(2)}) collective-permute-start(f32[4,2048]{1,0:T(4,128)S(1)} %broadcast_select_fusion.6), channel_id=1, source_target_pairs={{0,4},{4,8},{8,12},{12,16},{16,20},{20,24},{24,28},{1,5},{5,9},{9,... | collective-permute-start | bytes 98312 | tf_op jit(solution)/shard_map/ppermute | solution.py:15
  97.1 6.0 %collective-permute-start.9 = (f32[4,2048]{1,0:T(4,128)S(1)}, f32[4,2048]{1,0:T(4,128)S(1)}, u32[]{:S(2)}, u32[]{:S(2)}) collective-permute-start(f32[4,2048]{1,0:T(4,128)S(1)} %broadcast_select_fusion.5), channel_id=1, source_target_pairs={{4,0},{8,4},{12,8},{16,12},{20,16},{24,20},{28,24},{5,1},{9,5},{13... | collective-permute-start | bytes 98312 | tf_op jit(solution)/shard_map/ppermute | solution.py:15
where the time goes:
time: 200 us; the launch traced here: 199 us
  blocking collectives  48.2 us (24%)
  matrix products  43.1 us (22%)
  local copies, waits for them, and re-layouts  42.5 us (21%)
  starting transfers between devices  33 us (16%)
  other arithmetic  28.2 us (14%)
  waiting for transfers between devices  2.87 us (1%)
    psum x1, blocking collectives, on_device(): partial_grams.append(lax.psum(local_block, ('fx', 'fy')))  48.2 us
    dot_general x3, matrix products, contract(): jnp.einsum('fkab,fkbr->far', block_mats, shaped, precision=lax.Precision....  36 us
    ppermute x12, starting transfers between devices, from_behind(): return lax.ppermute(block, axis, route)  33 us
    reshape x3, local copies, waits for them, and re-layouts, contract(): shaped = picked.reshape(face_count, picked.shape[1], DOF, NRHS)  12.3 us
    another operation x3, other arithmetic, solve_small(): factor = jnp.linalg.cholesky(normal_matrix)  9.45 us
    gather x6, local copies, waits for them, and re-layouts, on_device(): jnp.take(extended, face_columns, axis=0)  8.18 us
    another operation x2, other arithmetic, solve_small(): coeffs = jax.scipy.linalg.cho_solve((factor, True), right_terms)  8.01 us
    select_n x4, other arithmetic, on_device(): jnp.take(extended, face_columns, axis=0)  7.51 us
  transfers between devices with their start and end apart: 12, of which 1 were waited for; matrix products, arithmetic and copies ran while one was open for 9% of the time, Pallas kernels for 0%

commit v1 on v0

--- a/solution.py
+++ b/solution.py
@@ -7,6 +7,11 @@
 NRHS = 32
 BLOCKS = 11
 POWERS = 3
+
+
+def move_arrays(row_data):
+    base_arr = lax.all_gather(row_data, axis_name=("fx", "fy")).sum(axis=0)
+    return base_arr
 
 
 def from_behind(block, axis, distance):
@@ -67,7 +72,7 @@
         local_block = jnp.dot(
             earlier_rows.T, as_rows(fields[-1]), precision=high, preferred_element_type=jnp.float32
         )
-        partial_grams.append(lax.psum(local_block, ("fx", "fy")))
+        partial_grams.append(move_arrays(local_block))
     total_cols = (POWERS + 1) * NRHS
     upper_part = jnp.concatenate(
         [

time: 200 us -> 307 us (1.53)
  blocking collectives: 48.2 us -> 169 us
  starting transfers between devices: 33 us -> 24 us
    all_gather x0 -> x4, blocking collectives: none -> 169 us  [move_arrays(): base_arr = lax.all_gather(row_data, axis_name=('fx', 'fy')).sum(axis=0)]
    psum x1 -> x0, blocking collectives: 48.2 us -> none  [on_device(): partial_grams.append(lax.psum(local_block, ('fx', 'fy')))]
    ppermute x12, starting transfers between devices: 33 us -> 24 us  [from_behind(): return lax.ppermute(block, axis, route)]
  transfers between devices with their start and end apart: 12 -> 12, of which waited for: 1 -> 0; matrix products, arithmetic and copies ran while one was open for 9% -> 5% of each run, Pallas kernels for 0% -> 0%
where the time goes in v1:
time: 307 us; the launch traced here: 306 us
  blocking collectives  169 us (55%)
  local copies, waits for them, and re-layouts  42.8 us (14%)
  matrix products  41.1 us (13%)
  other arithmetic  28.4 us (9%)
  starting transfers between devices  24 us (8%)
    all_gather x4, blocking collectives, move_arrays(): base_arr = lax.all_gather(row_data, axis_name=('fx', 'fy')).sum(axis=0)  169 us
    dot_general x3, matrix products, contract(): jnp.einsum('fkab,fkbr->far', block_mats, shaped, precision=lax.Precision....  36 us
    ppermute x12, starting transfers between devices, from_behind(): return lax.ppermute(block, axis, route)  24 us
    reshape x3, local copies, waits for them, and re-layouts, contract(): shaped = picked.reshape(face_count, picked.shape[1], DOF, NRHS)  12.3 us
    another operation x3, other arithmetic, solve_small(): factor = jnp.linalg.cholesky(normal_matrix)  9.45 us
    gather x6, local copies, waits for them, and re-layouts, on_device(): jnp.take(extended, face_columns, axis=0)  8.18 us
    another operation x2, other arithmetic, solve_small(): coeffs = jax.scipy.linalg.cho_solve((factor, True), right_terms)  8.01 us
    select_n x4, other arithmetic, on_device(): jnp.take(extended, face_columns, axis=0)  7.5 us
  transfers between devices with their start and end apart: 12, of which 0 were waited for; matrix products, arithmetic and copies ran while one was open for 5% of the time, Pallas kernels for 0%

profile of v1, /device:TPU:0, one launch (start us, length us, event | category | flops | bytes accessed | tf_op | source)
XLA Modules:
  0.0 306.2 jit_solution(14876177268641244859)
XLA Ops:
  0.6 0.8 compare_and_fusion.1
  1.5 1.5 gather_fusion
  3.1 4.9 %collective-permute-start = (f32[4,2048]{1,0:T(4,128)S(1)}, f32[4,2048]{1,0:T(4,128)S(1)}, u32[]{:S(2)}, u32[]{:S(2)}) collective-permute-start(f32[4,2048]{1,0:T(4,128)S(1)} %broadcast_select_fusion.14), channel_id=1, source_target_pairs={{0,4},{4,8},{8,12},{12,16},{16,20},{20,24},{24,28},{1,5},{5,9},{9,... | collective-permute-start | bytes 98312 | tf_op jit(solution)/shard_map/ppermute | solution.py:20
  7.9 1.5 gather_fusion.1
  9.5 1.3 collective-permute-start.1
  10.8 1.5 gather_fusion.2
  12.4 1.4 collective-permute-start.2
  13.9 1.5 gather_fusion.3
  15.4 1.3 collective-permute-start.3
  16.7 0.7 compare_select_fusion
  17.4 0.7 compare_and_fusion
  18.1 1.1 reshape.90
  19.3 5.7 %reshape.92 = f32[16,11,64,64]{3,2,0,1:T(8,128)} reshape(f32[16,11,4096]{2,0,1:T(8,128)} %param.9) | data formatting | bytes 5767168 | tf_op jit(solution)/shard_map/reshape | solution.py:57
  25.0 1.0 fusion.39
  26.0 47.2 %all-gather = f32[1024,32]{1,0:T(8,128)S(1)} all-gather(f32[32,32]{1,0:T(8,128)S(1)} %fusion.39), channel_id=2, replica_groups=mesh['fx'=8,'fy'=4] {'fx','fy'}, dimensions={0}, use_global_device_ids=true | all-gather | bytes 135168 | tf_op jit(solution)/shard_map/all_gather | solution.py:13
  73.4 1.2 gather_fusion.4
  74.6 1.5 reshape.258
  76.1 1.8 broadcast_select_fusion.2
  77.9 3.6 %reshape.286 = f32[16,11,64,32]{3,2,1,0:T(8,128)} reshape(f32[16,11,2048]{2,1,0:T(8,128)S(1)} %broadcast_select_fusion.2) | data formatting | bytes 2883584 | tf_op jit(solution)/shard_map/reshape | solution.py:33
  81.5 12.0 %fusion.6 = f32[16,64,32]{1,2,0:T(8,128)S(1)} fusion(f32[16,11,64,64]{3,2,0,1:T(8,128)} %reshape.92, f32[16,11,64,32]{3,2,1,0:T(8,128)} %reshape.286), kind=kOutput, calls=%fused_computation.21 | convolution fusion | flops 276824064 | bytes 4456448 | tf_op jit(solution)/shard_map/fkab,fkbr->far/dot_general | solution.py:34
  93.7 0.2 reshape.93
  93.9 0.6 gather_fusion.6
  94.5 0.6 gather_fusion.7
  95.1 0.6 gather_fusion.8
  95.7 0.6 gather_fusion.5
  96.5 1.3 collective-permute-start.5
  97.9 2.2 collective-permute-start.6
  100.2 1.3 collective-permute-start.7
  101.5 4.3 %collective-permute-start.4 = (f32[4,2048]{1,0:T(4,128)S(1)}, f32[4,2048]{1,0:T(4,128)S(1)}, u32[]{:S(2)}, u32[]{:S(2)}) collective-permute-start(f32[4,2048]{1,0:T(4,128)S(1)} %broadcast_select_fusion.10), channel_id=1, source_target_pairs={{0,4},{4,8},{8,12},{12,16},{16,20},{20,24},{24,28},{1,5},{5,9},{9,... | collective-permute-start | bytes 98312 | tf_op jit(solution)/shard_map/ppermute | solution.py:20
  106.1 0.5 convolution_bitcast_fusion.1
  106.6 40.3 %all-gather.4 = f32[32,64,32]{1,2,0:T(8,128)S(1)} all-gather(f32[1,64,32]{1,2,0:T(8,128)S(1)} %convolution_bitcast_fusion.1), channel_id=3, replica_groups=mesh['fx'=8,'fy'=4] {'fx','fy'}, dimensions={0}, use_global_device_ids=true | all-gather | bytes 270336 | tf_op jit(solution)/shard_map/all_gather | solution.py:13
  147.2 1.2 gather_fusion.9
  148.3 1.5 reshape.270
  149.9 1.8 broadcast_select_fusion.1
  151.7 3.6 %reshape.287 = f32[16,11,64,32]{3,2,1,0:T(8,128)} reshape(f32[16,11,2048]{2,1,0:T(8,128)S(1)} %broadcast_select_fusion.1) | data formatting | bytes 2883584 | tf_op jit(solution)/shard_map/reshape | solution.py:33
  155.2 12.0 %fusion.9 = f32[16,64,32]{1,2,0:T(8,128)S(1)} fusion(f32[16,11,64,64]{3,2,0,1:T(8,128)} %reshape.92, f32[16,11,64,32]{3,2,1,0:T(8,128)} %reshape.287), kind=kOutput, calls=%fused_computation.22 | convolution fusion | flops 276824064 | bytes 4456448 | tf_op jit(solution)/shard_map/fkab,fkbr->far/dot_general | solution.py:34
  167.7 0.6 gather_fusion.12
  168.3 0.6 gather_fusion.13
  168.9 0.6 gather_fusion.10
  169.4 0.6 gather_fusion.11
  170.3 2.2 collective-permute-start.10
  172.6 1.3 collective-permute-start.11
  173.9 1.3 collective-permute-start.8
  175.3 1.3 collective-permute-start.9
  176.9 0.6 convolution_bitcast_fusion
  177.6 42.9 %all-gather.5 = f32[32,96,32]{1,2,0:T(8,128)S(1)} all-gather(f32[1,96,32]{1,2,0:T(8,128)S(1)} %convolution_bitcast_fusion), channel_id=4, replica_groups=mesh['fx'=8,'fy'=4] {'fx','fy'}, dimensions={0}, use_global_device_ids=true | all-gather | bytes 405504 | tf_op jit(solution)/shard_map/all_gather | solution.py:13
  220.8 1.2 gather_fusion.14
  221.9 1.6 reshape.282
  223.6 3.2 %broadcast_select_fusion = f32[16,11,2048]{2,1,0:T(8,128)} fusion(f32[16,11,2048]{2,1,0:T(8,128)} %reshape.282, pred[16,11]{1,0:T(8,128)(4,1)S(1)} %compare_and_fusion), kind=kLoop, calls=%fused_computation.27 | loop fusion | flops 360448 | bytes 2883760 | tf_op jit(solution)/shard_map/jit(_take)/select_n | solution.py:70
  226.8 5.2 %reshape.288 = f32[16,11,64,32]{3,2,1,0:T(8,128)} reshape(f32[16,11,2048]{2,1,0:T(8,128)} %broadcast_select_fusion) | data formatting | bytes 2883584 | tf_op jit(solution)/shard_map/reshape | solution.py:33
  232.0 12.0 %fusion.12 = f32[16,64,32]{1,2,0:T(8,128)S(1)} fusion(f32[16,11,64,64]{3,2,0,1:T(8,128)} %reshape.92, f32[16,11,64,32]{3,2,1,0:T(8,128)} %reshape.288), kind=kOutput, calls=%fused_computation.23 | convolution fusion | flops 276824064 | bytes 4456448 | tf_op jit(solution)/shard_map/fkab,fkbr->far/dot_general | solution.py:34
  244.5 0.5 pad_maximum_fusion.1
  245.0 0.4 fusion.40
  245.4 38.3 %all-gather.3 = f32[4096,32]{0,1:T(8,128)S(1)} all-gather(f32[128,32]{0,1:T(8,128)S(1)} %fusion.40), channel_id=5, replica_groups=mesh['fx'=8,'fy'=4] {'fx','fy'}, dimensions={0}, use_global_device_ids=true | all-gather | bytes 540672 | tf_op jit(solution)/shard_map/all_gather | solution.py:13
  284.3 0.2 fusion.35
  284.8 0.2 fusion.30
  285.1 8.8 %cholesky.16 = f32[96,96]{1,0:T(8,128)S(1)} custom-call(f32[96,96]{1,0:T(8,128)S(1)} %fusion.29), custom_call_target="Cholesky" | custom-call | tf_op jit(solution)/shard_map/jit(cholesky)/cholesky | solution.py:49
  293.9 0.6 compare_reduce_fusion
  294.6 0.7 fusion.24
  295.2 7.4 %custom-call.10 = f32[1,96,96]{1,2,0:T(8,128)S(1)} custom-call(f32[1,96,96]{2,1,0:T(8,128)S(1)} %fusion.24), custom_call_target="InvertDiagBlocksLowerTriangular" | custom-call | tf_op jit(solution)/shard_map/jit(_cho_solve)/triangular_solve | solution.py:50
  303.1 0.8 fusion.38
  303.9 0.6 fusion.41
  304.5 0.9 reshape.98
  305.3 0.9 reshape.97
  (67 shorter events, 5.1 us)
Async XLA Ops:
  3.1 70.2 %collective-permute-start = (f32[4,2048]{1,0:T(4,128)S(1)}, f32[4,2048]{1,0:T(4,128)S(1)}, u32[]{:S(2)}, u32[]{:S(2)}) collective-permute-start(f32[4,2048]{1,0:T(4,128)S(1)} %broadcast_select_fusion.14), channel_id=1, source_target_pairs={{0,4},{4,8},{8,12},{12,16},{16,20},{20,24},{24,28},{1,5},{5,9},{9,... | collective-permute-start | bytes 98312 | tf_op jit(solution)/shard_map/ppermute | solution.py:20
  9.5 63.8 %collective-permute-start.1 = (f32[4,2048]{1,0:T(4,128)S(1)}, f32[4,2048]{1,0:T(4,128)S(1)}, u32[]{:S(2)}, u32[]{:S(2)}) collective-permute-start(f32[4,2048]{1,0:T(4,128)S(1)} %broadcast_select_fusion.13), channel_id=1, source_target_pairs={{4,0},{8,4},{12,8},{16,12},{20,16},{24,20},{28,24},{5,1},{9,5},{13... | collective-permute-start | bytes 98312 | tf_op jit(solution)/shard_map/ppermute | solution.py:20
  12.4 60.9 %collective-permute-start.2 = (f32[4,2048]{1,0:T(4,128)S(1)}, f32[4,2048]{1,0:T(4,128)S(1)}, u32[]{:S(2)}, u32[]{:S(2)}) collective-permute-start(f32[4,2048]{1,0:T(4,128)S(1)} %broadcast_select_fusion.12), channel_id=1, source_target_pairs={{0,1},{1,2},{2,3},{4,5},{5,6},{6,7},{8,9},{9,10},{10,11},{12,13},{... | collective-permute-start | bytes 98312 | tf_op jit(solution)/shard_map/ppermute | solution.py:20
  15.4 57.9 %collective-permute-start.3 = (f32[4,2048]{1,0:T(4,128)S(1)}, f32[4,2048]{1,0:T(4,128)S(1)}, u32[]{:S(2)}, u32[]{:S(2)}) collective-permute-start(f32[4,2048]{1,0:T(4,128)S(1)} %broadcast_select_fusion.11), channel_id=1, source_target_pairs={{1,0},{2,1},{3,2},{5,4},{6,5},{7,6},{9,8},{10,9},{11,10},{13,12},{... | collective-permute-start | bytes 98312 | tf_op jit(solution)/shard_map/ppermute | solution.py:20
  25.0 48.3 %copy-start = (f32[16,2048]{1,0:T(8,128)S(1)}, f32[16,2048]{1,0:T(8,128)}, u32[]{:S(2)}) copy-start(f32[16,2048]{1,0:T(8,128)} %param.8) | copy-start | bytes 393220
  96.5 50.6 %collective-permute-start.5 = (f32[4,2048]{1,0:T(4,128)S(1)}, f32[4,2048]{1,0:T(4,128)S(1)}, u32[]{:S(2)}, u32[]{:S(2)}) collective-permute-start(f32[4,2048]{1,0:T(4,128)S(1)} %broadcast_select_fusion.9), channel_id=1, source_target_pairs={{4,0},{8,4},{12,8},{16,12},{20,16},{24,20},{28,24},{5,1},{9,5},{13... | collective-permute-start | bytes 98312 | tf_op jit(solution)/shard_map/ppermute | solution.py:20
  97.9 49.2 %collective-permute-start.6 = (f32[4,2048]{1,0:T(4,128)S(1)}, f32[4,2048]{1,0:T(4,128)S(1)}, u32[]{:S(2)}, u32[]{:S(2)}) collective-permute-start(f32[4,2048]{1,0:T(4,128)S(1)} %broadcast_select_fusion.8), channel_id=1, source_target_pairs={{0,1},{1,2},{2,3},{4,5},{5,6},{6,7},{8,9},{9,10},{10,11},{12,13},{... | collective-permute-start | bytes 98312 | tf_op jit(solution)/shard_map/ppermute | solution.py:20
  100.2 46.9 %collective-permute-start.7 = (f32[4,2048]{1,0:T(4,128)S(1)}, f32[4,2048]{1,0:T(4,128)S(1)}, u32[]{:S(2)}, u32[]{:S(2)}) collective-permute-start(f32[4,2048]{1,0:T(4,128)S(1)} %broadcast_select_fusion.7), channel_id=1, source_target_pairs={{1,0},{2,1},{3,2},{5,4},{6,5},{7,6},{9,8},{10,9},{11,10},{13,12},{... | collective-permute-start | bytes 98312 | tf_op jit(solution)/shard_map/ppermute | solution.py:20
  101.5 45.5 %collective-permute-start.4 = (f32[4,2048]{1,0:T(4,128)S(1)}, f32[4,2048]{1,0:T(4,128)S(1)}, u32[]{:S(2)}, u32[]{:S(2)}) collective-permute-start(f32[4,2048]{1,0:T(4,128)S(1)} %broadcast_select_fusion.10), channel_id=1, source_target_pairs={{0,4},{4,8},{8,12},{12,16},{16,20},{20,24},{24,28},{1,5},{5,9},{9,... | collective-permute-start | bytes 98312 | tf_op jit(solution)/shard_map/ppermute | solution.py:20
  170.3 50.4 %collective-permute-start.10 = (f32[4,2048]{1,0:T(4,128)S(1)}, f32[4,2048]{1,0:T(4,128)S(1)}, u32[]{:S(2)}, u32[]{:S(2)}) collective-permute-start(f32[4,2048]{1,0:T(4,128)S(1)} %broadcast_select_fusion.4), channel_id=1, source_target_pairs={{0,1},{1,2},{2,3},{4,5},{5,6},{6,7},{8,9},{9,10},{10,11},{12,13},{... | collective-permute-start | bytes 98312 | tf_op jit(solution)/shard_map/ppermute | solution.py:20
  172.6 48.1 %collective-permute-start.11 = (f32[4,2048]{1,0:T(4,128)S(1)}, f32[4,2048]{1,0:T(4,128)S(1)}, u32[]{:S(2)}, u32[]{:S(2)}) collective-permute-start(f32[4,2048]{1,0:T(4,128)S(1)} %broadcast_select_fusion.3), channel_id=1, source_target_pairs={{1,0},{2,1},{3,2},{5,4},{6,5},{7,6},{9,8},{10,9},{11,10},{13,12},{... | collective-permute-start | bytes 98312 | tf_op jit(solution)/shard_map/ppermute | solution.py:20
  173.9 46.7 %collective-permute-start.8 = (f32[4,2048]{1,0:T(4,128)S(1)}, f32[4,2048]{1,0:T(4,128)S(1)}, u32[]{:S(2)}, u32[]{:S(2)}) collective-permute-start(f32[4,2048]{1,0:T(4,128)S(1)} %broadcast_select_fusion.6), channel_id=1, source_target_pairs={{0,4},{4,8},{8,12},{12,16},{16,20},{20,24},{24,28},{1,5},{5,9},{9,... | collective-permute-start | bytes 98312 | tf_op jit(solution)/shard_map/ppermute | solution.py:20
  175.3 45.4 %collective-permute-start.9 = (f32[4,2048]{1,0:T(4,128)S(1)}, f32[4,2048]{1,0:T(4,128)S(1)}, u32[]{:S(2)}, u32[]{:S(2)}) collective-permute-start(f32[4,2048]{1,0:T(4,128)S(1)} %broadcast_select_fusion.5), channel_id=1, source_target_pairs={{4,0},{8,4},{12,8},{16,12},{20,16},{24,20},{28,24},{5,1},{9,5},{13... | collective-permute-start | bytes 98312 | tf_op jit(solution)/shard_map/ppermute | solution.py:20
